TPU v7x, 32 devices: a whole 2x2x4 slice. The times are simulated.
32 devices in a mesh: groups: 2 (over x), space: 16 (over z, y, core).
Axes of the slice: x: 2, y: 2, z: 4, core: 2. Of those that a mesh axis runs over, the one named last changes fastest.
Arguments:
- eigvecs: bfloat16 [32, 64, 2, 3, 128], P('groups', 'space'), parts along dimension 0, may hold values from -1.3515625 to 1.3515625
- phase_index: int32 [128], P('groups'), parts along dimension 0, may hold values from 0 to 47
- perambulator: bfloat16 [512, 2, 128, 128], P(('groups', 'space')), parts along dimension 0, may hold values from -0.046875 to 0.046875
- tile_sink: int32 [512, 1], P(('groups', 'space')), parts along dimension 0, may hold values from 0 to 15; in each aligned block of 16 rows (0 to 15, 16 to 31, ...) at most 2 rows name the same one
- tile_sep: int32 [512], P(('groups', 'space')), parts along dimension 0, may hold values from 0 to 7
- tile_diagram: int32 [512], P(('groups', 'space')), parts along dimension 0, may hold values from 0 to 1
Outputs:
- elementals: bfloat16 [32, 2, 128, 128], P(('groups', 'space')), parts along dimension 0
- correlator: float32 [512, 2], P(('groups', 'space')), parts along dimension 0
There are 2 independent parts, one for each index of `groups`. A program takes and returns all parts, laid end to end along the dimension named above; each array names one. Nothing has to cross between parts.
Inputs may be any that keep to these rules, and one draw needn't show every extreme that they name: `tile_sink`: in the tiles of one device no sink time is named by more than 2 tiles.
All inputs are finite; a program needn't handle non-finite values.
Results may differ from a plain program's by a relative error of at most 0.0048.
Values may be sent and summed in bfloat16 or wider, within the bound.
A program may use at most 128 MiB of HBM per device.

v0:
```python
import math
import jax
import jax.numpy as jnp
from jax import lax
from jax.sharding import PartitionSpec as P

PERIOD = 48


def make_right(vecs, cosine, sine):
    real_part = vecs[..., 0, :, :].astype(jnp.float32)
    imag_part = vecs[..., 1, :, :].astype(jnp.float32)
    cos_col = cosine[:, None, None]
    sin_col = sine[:, None, None]
    first = (cos_col * real_part - sin_col * imag_part).astype(jnp.bfloat16)
    second = (sin_col * real_part + cos_col * imag_part).astype(jnp.bfloat16)
    top = jnp.stack([first, second], -2)
    bottom = jnp.stack([second, -first], -2)
    return jnp.stack([top, bottom], -4)


def phases(indices):
    angle = 2.0 * math.pi / PERIOD * indices.astype(jnp.float32)
    return (jnp.cos(angle), jnp.sin(angle))


def contract_tiles(sink_mat, source_mat, tiles, diagram):

    def mult(left, right):
        return jnp.einsum("bij,bjk->bik", left, right, preferred_element_type=jnp.float32)

    tile_re = tiles[:, 0]
    tile_im = tiles[:, 1]
    trans_re = jnp.swapaxes(tile_re, 1, 2)
    trans_im = -jnp.swapaxes(tile_im, 1, 2)
    flag = (diagram == 1)[:, None, None]
    left_re = jnp.where(flag, trans_re, tile_re)
    left_im = jnp.where(flag, trans_im, tile_im)
    right_re = jnp.where(flag, tile_re, trans_re)
    right_im = jnp.where(flag, tile_im, trans_im)
    sink_re = sink_mat[:, 0]
    sink_im = sink_mat[:, 1]
    src_re = jnp.swapaxes(source_mat[:, 0], 1, 2)
    src_im = -jnp.swapaxes(source_mat[:, 1], 1, 2)
    first_re = mult(sink_re, left_re) - mult(sink_im, left_im)
    first_im = mult(sink_re, left_im) + mult(sink_im, left_re)
    second_re = jnp.swapaxes(mult(src_re, right_re) - mult(src_im, right_im), 1, 2)
    second_im = jnp.swapaxes(mult(src_re, right_im) + mult(src_im, right_re), 1, 2)
    trace_re = jnp.sum(first_re * second_re - first_im * second_im, axis=(1, 2))
    trace_im = jnp.sum(first_re * second_im + first_im * second_re, axis=(1, 2))
    return jnp.stack([trace_re, trace_im], -1)


def run_blocks(step_fn, items, total):
    block = math.gcd(32, total)
    shaped = tuple((item.reshape((total // block, block) + item.shape[1:]) for item in items))
    result = lax.map(step_fn, shaped)
    return result.reshape((total,) + result.shape[2:])


def local(eigvecs, phase_index, perambulator, tile_sink, tile_sep, tile_diagram):
    tile_count = perambulator.shape[0]
    sinks = tile_sink[:, 0]
    cosine, sine = phases(phase_index)
    slices = lax.all_to_all(eigvecs, "space", split_axis=0, concat_axis=1, tiled=True)
    vecs = slices[0]
    right = make_right(vecs, cosine, sine)
    value = jnp.einsum("spck,spcol->okl", vecs, right, preferred_element_type=jnp.float32)
    elemental = value.astype(jnp.bfloat16)[None]
    gathered = lax.all_gather(elemental, "space", axis=0, tiled=True)
    time_count = gathered.shape[0]
    sources = jnp.mod(sinks - tile_sep, time_count)

    def holder_block(items):
        tiles, sink_ids, source_ids, diagram = items
        return contract_tiles(gathered[sink_ids], gathered[source_ids], tiles, diagram)

    correlator = run_blocks(holder_block, (perambulator, sinks, sources, tile_diagram), tile_count)
    return (elemental, correlator)


def solution(mesh):
    return jax.shard_map(
        local,
        mesh=mesh,
        in_specs=(
            P("groups", "space", None, None, None),
            P("groups"),
            P(("groups", "space"), None, None, None),
            P(("groups", "space"), None),
            P(("groups", "space")),
            P(("groups", "space")),
        ),
        out_specs=(P(("groups", "space"), None, None, None), P(("groups", "space"), None)),
        check_vma=False,
    )
```

profile of v0, /device:TPU:0, one launch (start us, length us, event | category | flops | bytes accessed | tf_op | source)
XLA Modules:
  0.0 76.8 jit_solution(16801960626893713510)
XLA Ops:
  7.2 7.6 %all-to-all-start = ((bf16[16,4,2,3,128]{4,2,3,1,0:T(2,128)(2,1)}), bf16[16,4,2,3,128]{4,2,3,1,0:T(2,128)(2,1)S(1)}, u32[]{:S(2)}, u32[]{:S(2)}) async-start(bf16[16,4,2,3,128]{4,2,3,1,0:T(2,128)(2,1)} %param.6), calls=%async_computation | async-start | bytes 196608 | tf_op jit(solution)/shard_map/all_to_all | solution.py:65
  14.9 7.3 %all-to-all-done = bf16[16,4,2,3,128]{4,2,3,1,0:T(2,128)(2,1)S(1)} async-done(((bf16[16,4,2,3,128]{4,2,3,1,0:T(2,128)(2,1)}), bf16[16,4,2,3,128]{4,2,3,1,0:T(2,128)(2,1)S(1)}, u32[]{:S(2)}, u32[]{:S(2)}) %all-to-all-start) | async-done | bytes 98336 | tf_op jit(solution)/shard_map/all_to_all | solution.py:65
  22.3 0.1 fusion.21
  22.4 0.3 fusion
  22.6 0.7 copy.37
  23.5 0.3 copy.40
  23.8 0.3 copy.42
  24.1 0.4 copy-done.4
  24.5 0.6 copy-done.3
  25.2 0.6 copy-done.5
  25.8 0.7 copy.49
  26.5 32.4 %all-gather.3.cloned.1.call-done = bf16[32,128,128]{2,1,0:T(8,128)(2,1)} async-done(((bf16[2,128,128]{2,1,0:T(8,128)(2,1)}), bf16[32,128,128]{2,1,0:T(8,128)(2,1)}) %all-gather.3.cloned.1.call-update) | async-done | bytes 1048592 | tf_op jit(solution)/shard_map/all_gather | solution.py:70
  59.0 2.9 %gather_fusion.1 = bf16[16,2,128,128]{3,2,1,0:T(8,128)(2,1)} fusion(bf16[16,2,128,128]{3,2,1,0:T(8,128)(2,1)} %bitcast.124, s32[1024]{0:T(1024)S(1)} %pad_clamp_fusion), kind=kCustom, calls=%fused_computation.1 | custom fusion | bytes 2097216 | tf_op jit(solution)/shard_map/while/body/eval_jaxpr/gather | solution.py:76
  61.9 2.0 %gather_fusion = bf16[16,2,128,128]{3,2,1,0:T(8,128)(2,1)S(1)} fusion(bf16[16,2,128,128]{3,2,1,0:T(8,128)(2,1)} %bitcast.125, s32[1024]{0:T(1024)S(1)} %pad_clamp_fusion.1), kind=kCustom, calls=%fused_computation | custom fusion | bytes 2097216 | tf_op jit(solution)/shard_map/while/body/eval_jaxpr/gather | solution.py:76
  63.9 1.5 %fusion.5 = f32[16,128,128]{2,1,0:T(8,128)S(1)} fusion(bf16[16,2,128,128]{3,2,1,0:T(8,128)(2,1)} %gather_fusion.1, pred[16]{0:T(512)(128)(4,1)S(1)} %broadcast_compare_fusion, bf16[16,128,128]{1,2,0:T(8,128)(2,1)S(1)} %copy.42, bf16[16,2,128,128]{3,2,1,0:T(8,128)(2,1)S(1)} %copy-done), kind=kOutput, calls=%fused_computation.24 | convolution fusion | flops 67633152 | bytes 2621952 | tf_op jit(solution)/shard_map/while/body/eval_jaxpr/bij,bjk->bik/dot_general | solution.py:30
  65.4 0.4 fusion.3
  65.7 0.8 %copy-done.1 = bf16[16,2,128,128]{3,2,1,0:T(8,128)(2,1)S(1)} copy-done((bf16[16,2,128,128]{3,2,1,0:T(8,128)(2,1)S(1)}, bf16[16,2,128,128]{3,2,1,0:T(8,128)(2,1)}, u32[]{:S(2)}) %copy-start.1) | copy-done | bytes 1048600
  66.6 0.4 fusion.6
  67.0 0.4 fusion.4
  67.4 0.4 convolution_add_fusion
  67.8 0.4 convolution_subtract_fusion
  68.2 0.4 convolution_subtract_fusion.1
  68.6 0.7 subtract_reduce_fusion
  69.3 0.6 pad_maximum_fusion
  (20 shorter events, 0.4 us)
Async XLA Ops:
  7.2 7.6 %copy-start.2 = (s32[64]{0:T(128)S(1)}, s32[64]{0:T(128)}, u32[]{:S(2)}) copy-start(s32[64]{0:T(128)} %param.7) | copy-start | bytes 772
  7.2 16.3 %copy-start = (bf16[16,2,128,128]{3,2,1,0:T(8,128)(2,1)S(1)}, bf16[16,2,128,128]{3,2,1,0:T(8,128)(2,1)}, u32[]{:S(2)}) copy-start(bf16[16,2,128,128]{3,2,1,0:T(8,128)(2,1)} %param.8) | copy-start | bytes 3145732
  7.2 14.9 %all-to-all-start = ((bf16[16,4,2,3,128]{4,2,3,1,0:T(2,128)(2,1)}), bf16[16,4,2,3,128]{4,2,3,1,0:T(2,128)(2,1)S(1)}, u32[]{:S(2)}, u32[]{:S(2)}) async-start(bf16[16,4,2,3,128]{4,2,3,1,0:T(2,128)(2,1)} %param.6), calls=%async_computation | async-start | bytes 196608 | tf_op jit(solution)/shard_map/all_to_all | solution.py:65
  14.7 44.2 %all-gather.3.cloned.1.call-start = ((), (), s32[]{:S(2)}) async-start(), calls=%async_computation.1 | async-start | bytes 1114112 | tf_op jit(solution)/shard_map/all_gather | solution.py:70
  23.8 0.7 copy-start.4
  24.5 0.7 copy-start.3
  25.1 0.7 copy-start.5
  65.3 1.2 %copy-start.1 = (bf16[16,2,128,128]{3,2,1,0:T(8,128)(2,1)S(1)}, bf16[16,2,128,128]{3,2,1,0:T(8,128)(2,1)}, u32[]{:S(2)}) copy-start(bf16[16,2,128,128]{3,2,1,0:T(8,128)(2,1)} %gather_fusion.1) | copy-start | bytes 3145732
Sparse Core Ops, SparseCore 0:
  23.5 35.3 all-gather.2
where the time goes:
time: 77.1 us; the launch traced here: 76.8 us
  waiting for transfers between devices  39.7 us (51%)
  between operations  14.2 us (18%)
  local copies, waits for them, and re-layouts  9.55 us (12%)
  starting transfers between devices  7.6 us (10%)
  matrix products  4.81 us (6%)
  other arithmetic  0.85 us (1%)
    all_gather x1, waiting for transfers between devices, local(): gathered = lax.all_gather(elemental, 'space', axis=0, tiled=True)  32.4 us
    all_to_all x1, starting transfers between devices, local(): lax.all_to_all(eigvecs, 'space', split_axis=0, concat_axis=1, tiled=True)  7.56 us
    all_to_all x1, waiting for transfers between devices, local(): lax.all_to_all(eigvecs, 'space', split_axis=0, concat_axis=1, tiled=True)  7.27 us
    dot_general x8, matrix products, mult(): jnp.einsum('bij,bjk->bik', left, right, preferred_element_type=jnp.float32)  4.56 us
    unnamed x13, local copies, waits for them, and re-layouts  3.24 us
    gather x1, local copies, waits for them, and re-layouts, holder_block(): gathered[source_ids]  2.92 us
    gather x1, local copies, waits for them, and re-layouts, holder_block(): gathered[sink_ids]  1.97 us
  transfers between devices with their start and end apart: 2, of which 2 were waited for; matrix products, arithmetic and copies ran while one was open for 2% of the time, Pallas kernels for 0%

commit v1 on v0

--- a/solution.py
+++ b/solution.py
@@ -67,7 +67,23 @@
     right = make_right(vecs, cosine, sine)
     value = jnp.einsum("spck,spcol->okl", vecs, right, preferred_element_type=jnp.float32)
     elemental = value.astype(jnp.bfloat16)[None]
-    gathered = lax.all_gather(elemental, "space", axis=0, tiled=True)
+    ways, here, turn = (lax.axis_size("space"), lax.axis_index("space"), elemental.shape[0])
+    shape = [n * ways if d == 0 else n for d, n in enumerate(elemental.shape)]
+    full = lax.dynamic_update_slice_in_dim(
+        jnp.zeros(shape, elemental.dtype), elemental, here * turn, axis=0
+    )
+    going_up = going_down = elemental
+    for far in range(1, ways // 2 + 1):
+        going_up = lax.ppermute(going_up, "space", [(d, (d + 1) % ways) for d in range(ways)])
+        full = lax.dynamic_update_slice_in_dim(full, going_up, (here - far) % ways * turn, axis=0)
+        if 2 * far < ways:
+            going_down = lax.ppermute(
+                going_down, "space", [(d, (d - 1) % ways) for d in range(ways)]
+            )
+            full = lax.dynamic_update_slice_in_dim(
+                full, going_down, (here + far) % ways * turn, axis=0
+            )
+    gathered = full
     time_count = gathered.shape[0]
     sources = jnp.mod(sinks - tile_sep, time_count)
 

time: 77.1 us -> 81.7 us (1.060)
  between operations: 14.2 us -> 1.42 us
  waiting for transfers between devices: 39.7 us -> 50.7 us
  starting transfers between devices: 7.6 us -> 12.5 us
  local copies, waits for them, and re-layouts: 9.55 us -> 11.1 us
    ppermute x0 -> x15, waiting for transfers between devices: none -> 48.2 us  [the longest x8 48.2 us: local(): lax.ppermute(going_up, 'space', [(d, (d + 1) % ways) for d in range(ways)])]
    all_gather x1 -> x0, waiting for transfers between devices: 32.4 us -> none  [local(): gathered = lax.all_gather(elemental, 'space', axis=0, tiled=True)]
    ppermute x0 -> x15, starting transfers between devices: none -> 5.06 us  [the longest x8 3.04 us: local(): lax.ppermute(going_up, 'space', [(d, (d + 1) % ways) for d in range(ways)])]
    all_to_all x1, waiting for transfers between devices: 7.27 us -> 2.49 us  [local(): lax.all_to_all(eigvecs, 'space', split_axis=0, concat_axis=1, tiled=True)]
    ppermute x0 -> x15, local copies, waits for them, and re-layouts: none -> 1.78 us  [the longest x8 0.95 us: local(): lax.ppermute(going_up, 'space', [(d, (d + 1) % ways) for d in range(ways)])]
    gather x1, local copies, waits for them, and re-layouts: 2.92 us -> 1.67 us  [holder_block(): gathered[source_ids]]
    squeeze x2, local copies, waits for them, and re-layouts: 0.35 us -> 1.56 us  [contract_tiles(): tile_re = tiles[:, 0]]
    unnamed x13 -> x17, local copies, waits for them, and re-layouts: 3.24 us -> 3.57 us
  transfers between devices with their start and end apart: 2 -> 16, of which waited for: 2 -> 9; matrix products, arithmetic and copies ran while one was open for 2% -> 4% of each run, Pallas kernels for 0% -> 0%
where the time goes in v1:
time: 81.7 us; the launch traced here: 81.4 us
  waiting for transfers between devices  50.7 us (62%)
  starting transfers between devices  12.5 us (15%)
  local copies, waits for them, and re-layouts  11.1 us (14%)
  matrix products  4.9 us (6%)
  between operations  1.42 us (2%)
  other arithmetic  0.85 us (1%)
    ppermute x8, waiting for transfers between devices, local(): lax.ppermute(going_up, 'space', [(d, (d + 1) % ways) for d in range(ways)])  48.2 us
    all_to_all x1, starting transfers between devices, local(): lax.all_to_all(eigvecs, 'space', split_axis=0, concat_axis=1, tiled=True)  7.43 us
    dot_general x8, matrix products, mult(): jnp.einsum('bij,bjk->bik', left, right, preferred_element_type=jnp.float32)  4.64 us
    unnamed x17, local copies, waits for them, and re-layouts  3.57 us
    ppermute x8, starting transfers between devices, local(): lax.ppermute(going_up, 'space', [(d, (d + 1) % ways) for d in range(ways)])  3.04 us
    all_to_all x1, waiting for transfers between devices, local(): lax.all_to_all(eigvecs, 'space', split_axis=0, concat_axis=1, tiled=True)  2.49 us
    ppermute x7, starting transfers between devices, local(): lax.ppermute(going_down, 'space', [(d, (d - 1) % ways) for d in range(way...  2.02 us
    gather x1, local copies, waits for them, and re-layouts, holder_block(): gathered[source_ids]  1.67 us
  transfers between devices with their start and end apart: 16, of which 9 were waited for; matrix products, arithmetic and copies ran while one was open for 4% of the time, Pallas kernels for 0%

profile of v1, /device:TPU:0, one launch (start us, length us, event | category | flops | bytes accessed | tf_op | source)
XLA Modules:
  0.0 81.4 jit_solution(2651674202723037139)
XLA Ops:
  0.6 7.4 %all-to-all-start = ((bf16[16,4,2,3,128]{4,2,3,1,0:T(2,128)(2,1)}), bf16[16,4,2,3,128]{4,2,3,1,0:T(2,128)(2,1)S(1)}, u32[]{:S(2)}, u32[]{:S(2)}) async-start(bf16[16,4,2,3,128]{4,2,3,1,0:T(2,128)(2,1)} %param.6), calls=%async_computation | async-start | bytes 196608 | tf_op jit(solution)/shard_map/all_to_all | solution.py:65
  8.3 0.6 copy-done.5
  9.0 0.6 copy-done.4
  9.6 0.6 copy-done.6
  10.3 1.3 %slice_bitcast_fusion.5 = (bf16[16,128,128]{2,1,0:T(8,128)(2,1)S(1)}, bf16[16,128,128]{2,1,0:T(8,128)(2,1)S(1)}) fusion(bf16[16,2,128,128]{3,2,1,0:T(8,128)(2,1)} %param.8), kind=kLoop, calls=%fused_computation.22 | loop fusion | bytes 2097152 | tf_op jit(solution)/shard_map/while/body/eval_jaxpr/squeeze | solution.py:32
  12.3 0.6 copy-done.7
  13.0 2.5 %all-to-all-done = bf16[16,4,2,3,128]{4,2,3,1,0:T(2,128)(2,1)S(1)} async-done(((bf16[16,4,2,3,128]{4,2,3,1,0:T(2,128)(2,1)}), bf16[16,4,2,3,128]{4,2,3,1,0:T(2,128)(2,1)S(1)}, u32[]{:S(2)}, u32[]{:S(2)}) %all-to-all-start) | async-done | bytes 98336 | tf_op jit(solution)/shard_map/all_to_all | solution.py:65
  16.1 1.7 %collective-permute-start.1 = (bf16[1,2,128,128]{2,3,1,0:T(8,128)(2,1)S(1)}, bf16[1,2,128,128]{2,3,1,0:T(8,128)(2,1)S(1)}, u32[]{:S(2)}, u32[]{:S(2)}) collective-permute-start(bf16[1,2,128,128]{2,3,1,0:T(8,128)(2,1)S(1)} %fusion.1), channel_id=1, source_target_pairs={{0,15},{1,0},{2,1},{3,2},{4,3},{5,4},{6,5},{7,6},{8,7},{9,8},{10,9... | collective-permute-start | bytes 196616 | tf_op jit(solution)/shard_map/ppermute | solution.py:80
  18.1 6.2 %collective-permute-done = bf16[1,2,128,128]{2,3,1,0:T(8,128)(2,1)S(1)} collective-permute-done((bf16[1,2,128,128]{2,3,1,0:T(8,128)(2,1)S(1)}, bf16[1,2,128,128]{2,3,1,0:T(8,128)(2,1)S(1)}, u32[]{:S(2)}, u32[]{:S(2)}) %collective-permute-start) | collective-permute-done | bytes 65568 | tf_op jit(solution)/shard_map/ppermute | solution.py:77
  24.6 0.5 collective-permute-start.2
  25.1 6.0 %collective-permute-done.2 = bf16[1,2,128,128]{2,3,1,0:T(8,128)(2,1)S(1)} collective-permute-done((bf16[1,2,128,128]{2,3,1,0:T(8,128)(2,1)S(1)}, bf16[1,2,128,128]{2,3,1,0:T(8,128)(2,1)S(1)}, u32[]{:S(2)}, u32[]{:S(2)}) %collective-permute-start.2) | collective-permute-done | bytes 65568 | tf_op jit(solution)/shard_map/ppermute | solution.py:77
  31.9 6.0 %collective-permute-done.4 = bf16[1,2,128,128]{2,3,1,0:T(8,128)(2,1)S(1)} collective-permute-done((bf16[1,2,128,128]{2,3,1,0:T(8,128)(2,1)S(1)}, bf16[1,2,128,128]{2,3,1,0:T(8,128)(2,1)S(1)}, u32[]{:S(2)}, u32[]{:S(2)}) %collective-permute-start.4) | collective-permute-done | bytes 65568 | tf_op jit(solution)/shard_map/ppermute | solution.py:77
  38.8 6.0 %collective-permute-done.6 = bf16[1,2,128,128]{2,3,1,0:T(8,128)(2,1)S(1)} collective-permute-done((bf16[1,2,128,128]{2,3,1,0:T(8,128)(2,1)S(1)}, bf16[1,2,128,128]{2,3,1,0:T(8,128)(2,1)S(1)}, u32[]{:S(2)}, u32[]{:S(2)}) %collective-permute-start.6) | collective-permute-done | bytes 65568 | tf_op jit(solution)/shard_map/ppermute | solution.py:77
  45.6 6.0 %collective-permute-done.8 = bf16[1,2,128,128]{2,3,1,0:T(8,128)(2,1)S(1)} collective-permute-done((bf16[1,2,128,128]{2,3,1,0:T(8,128)(2,1)S(1)}, bf16[1,2,128,128]{2,3,1,0:T(8,128)(2,1)S(1)}, u32[]{:S(2)}, u32[]{:S(2)}) %collective-permute-start.8) | collective-permute-done | bytes 65568 | tf_op jit(solution)/shard_map/ppermute | solution.py:77
  52.5 6.0 %collective-permute-done.10 = bf16[1,2,128,128]{2,3,1,0:T(8,128)(2,1)S(1)} collective-permute-done((bf16[1,2,128,128]{2,3,1,0:T(8,128)(2,1)S(1)}, bf16[1,2,128,128]{2,3,1,0:T(8,128)(2,1)S(1)}, u32[]{:S(2)}, u32[]{:S(2)}) %collective-permute-start.10) | collective-permute-done | bytes 65568 | tf_op jit(solution)/shard_map/ppermute | solution.py:77
  58.8 0.5 collective-permute-start.12
  59.3 5.9 %collective-permute-done.12 = bf16[1,2,128,128]{2,3,1,0:T(8,128)(2,1)S(1)} collective-permute-done((bf16[1,2,128,128]{2,3,1,0:T(8,128)(2,1)S(1)}, bf16[1,2,128,128]{2,3,1,0:T(8,128)(2,1)S(1)}, u32[]{:S(2)}, u32[]{:S(2)}) %collective-permute-start.12) | collective-permute-done | bytes 65568 | tf_op jit(solution)/shard_map/ppermute | solution.py:77
  65.6 6.2 %collective-permute-done.14 = bf16[1,2,128,128]{2,3,1,0:T(8,128)(2,1)S(1)} collective-permute-done((bf16[1,2,128,128]{2,3,1,0:T(8,128)(2,1)S(1)}, bf16[1,2,128,128]{2,3,1,0:T(8,128)(2,1)S(1)}, u32[]{:S(2)}, u32[]{:S(2)}) %collective-permute-start.14) | collective-permute-done | bytes 65568 | tf_op jit(solution)/shard_map/ppermute | solution.py:77
  71.9 1.7 %gather_fusion.1 = bf16[16,2,128,128]{3,2,1,0:T(8,128)(2,1)} fusion(bf16[16,2,128,128]{3,2,1,0:T(8,128)(2,1)S(1)} %constant_dynamic-update-slice_fusion, s32[1024]{0:T(1024)S(1)} %pad_clamp_fusion), kind=kCustom, calls=%fused_computation.1 | custom fusion | bytes 2097216 | tf_op jit(solution)/shard_map/while/body/eval_jaxpr/gather | solution.py:92
  73.6 1.7 %gather_fusion = bf16[16,2,128,128]{3,2,1,0:T(8,128)(2,1)} fusion(bf16[16,2,128,128]{3,2,1,0:T(8,128)(2,1)S(1)} %constant_dynamic-update-slice_fusion, s32[1024]{0:T(1024)S(1)} %pad_clamp_fusion.1), kind=kCustom, calls=%fused_computation | custom fusion | bytes 2097216 | tf_op jit(solution)/shard_map/while/body/eval_jaxpr/gather | solution.py:92
  75.3 1.5 %fusion.6 = f32[16,128,128]{2,1,0:T(8,128)S(1)} fusion(bf16[16,2,128,128]{3,2,1,0:T(8,128)(2,1)} %gather_fusion.1, pred[16]{0:T(512)(128)(4,1)S(1)} %broadcast_compare_fusion, bf16[16,128,128]{1,2,0:T(8,128)(2,1)S(1)} %copy.42, bf16[16,2,128,128]{3,2,1,0:T(8,128)(2,1)S(1)} %copy-done), kind=kOutput, calls=%fused_computation.25 | convolution fusion | flops 67633152 | bytes 2621952 | tf_op jit(solution)/shard_map/while/body/eval_jaxpr/bij,bjk->bik/dot_general | solution.py:30
  77.2 0.8 %copy-done.2 = bf16[16,2,128,128]{3,2,1,0:T(8,128)(2,1)S(1)} copy-done((bf16[16,2,128,128]{3,2,1,0:T(8,128)(2,1)S(1)}, bf16[16,2,128,128]{3,2,1,0:T(8,128)(2,1)}, u32[]{:S(2)}) %copy-start.2) | copy-done | bytes 1048600
  80.1 0.7 subtract_reduce_fusion
  80.8 0.6 pad_maximum_fusion
  (82 shorter events, 8.4 us)
Async XLA Ops:
  0.6 14.8 %all-to-all-start = ((bf16[16,4,2,3,128]{4,2,3,1,0:T(2,128)(2,1)}), bf16[16,4,2,3,128]{4,2,3,1,0:T(2,128)(2,1)S(1)}, u32[]{:S(2)}, u32[]{:S(2)}) async-start(bf16[16,4,2,3,128]{4,2,3,1,0:T(2,128)(2,1)} %param.6), calls=%async_computation | async-start | bytes 196608 | tf_op jit(solution)/shard_map/all_to_all | solution.py:65
  8.3 0.7 copy-start.5
  9.0 0.7 copy-start.4
  9.6 0.7 copy-start.6
  12.3 0.7 copy-start.7
  16.1 1.9 %copy-start.3 = (bf16[1,2,128,128]{3,2,1,0:T(8,128)(2,1)}, bf16[1,2,128,128]{3,2,1,0:T(8,128)(2,1)S(1)}, u32[]{:S(2)}) copy-start(bf16[1,2,128,128]{3,2,1,0:T(8,128)(2,1)S(1)} %copy.49) | copy-start | bytes 196612
  16.1 8.3 %collective-permute-start.1 = (bf16[1,2,128,128]{2,3,1,0:T(8,128)(2,1)S(1)}, bf16[1,2,128,128]{2,3,1,0:T(8,128)(2,1)S(1)}, u32[]{:S(2)}, u32[]{:S(2)}) collective-permute-start(bf16[1,2,128,128]{2,3,1,0:T(8,128)(2,1)S(1)} %fusion.1), channel_id=1, source_target_pairs={{0,15},{1,0},{2,1},{3,2},{4,3},{5,4},{6,5},{7,6},{8,7},{9,8},{10,9... | collective-permute-start | bytes 196616 | tf_op jit(solution)/shard_map/ppermute | solution.py:80
  17.8 6.5 %collective-permute-start = (bf16[1,2,128,128]{2,3,1,0:T(8,128)(2,1)S(1)}, bf16[1,2,128,128]{2,3,1,0:T(8,128)(2,1)S(1)}, u32[]{:S(2)}, u32[]{:S(2)}) collective-permute-start(bf16[1,2,128,128]{2,3,1,0:T(8,128)(2,1)S(1)} %fusion.1), channel_id=1, source_target_pairs={{0,1},{1,2},{2,3},{3,4},{4,5},{5,6},{6,7},{7,8},{8,9},{9,10},{10,1... | collective-permute-start | bytes 196616 | tf_op jit(solution)/shard_map/ppermute | solution.py:77
  24.5 6.7 %collective-permute-start.3 = (bf16[1,2,128,128]{2,3,1,0:T(8,128)(2,1)S(1)}, bf16[1,2,128,128]{2,3,1,0:T(8,128)(2,1)S(1)}, u32[]{:S(2)}, u32[]{:S(2)}) collective-permute-start(bf16[1,2,128,128]{2,3,1,0:T(8,128)(2,1)S(1)} %collective-permute-done.1), channel_id=1, source_target_pairs={{0,15},{1,0},{2,1},{3,2},{4,3},{5,4},{6,5},{7,6},{8,7},{9,8},{10,9... | collective-permute-start | bytes 196616 | tf_op jit(solution)/shard_map/ppermute | solution.py:80
  24.6 6.5 %collective-permute-start.2 = (bf16[1,2,128,128]{2,3,1,0:T(8,128)(2,1)S(1)}, bf16[1,2,128,128]{2,3,1,0:T(8,128)(2,1)S(1)}, u32[]{:S(2)}, u32[]{:S(2)}) collective-permute-start(bf16[1,2,128,128]{2,3,1,0:T(8,128)(2,1)S(1)} %collective-permute-done), channel_id=1, source_target_pairs={{0,1},{1,2},{2,3},{3,4},{4,5},{5,6},{6,7},{7,8},{8,9},{9,10},{10,1... | collective-permute-start | bytes 196616 | tf_op jit(solution)/shard_map/ppermute | solution.py:77
  31.4 6.7 %collective-permute-start.5 = (bf16[1,2,128,128]{2,3,1,0:T(8,128)(2,1)S(1)}, bf16[1,2,128,128]{2,3,1,0:T(8,128)(2,1)S(1)}, u32[]{:S(2)}, u32[]{:S(2)}) collective-permute-start(bf16[1,2,128,128]{2,3,1,0:T(8,128)(2,1)S(1)} %collective-permute-done.3), channel_id=1, source_target_pairs={{0,15},{1,0},{2,1},{3,2},{4,3},{5,4},{6,5},{7,6},{8,7},{9,8},{10,9... | collective-permute-start | bytes 196616 | tf_op jit(solution)/shard_map/ppermute | solution.py:80
  31.4 6.5 %collective-permute-start.4 = (bf16[1,2,128,128]{2,3,1,0:T(8,128)(2,1)S(1)}, bf16[1,2,128,128]{2,3,1,0:T(8,128)(2,1)S(1)}, u32[]{:S(2)}, u32[]{:S(2)}) collective-permute-start(bf16[1,2,128,128]{2,3,1,0:T(8,128)(2,1)S(1)} %collective-permute-done.2), channel_id=1, source_target_pairs={{0,1},{1,2},{2,3},{3,4},{4,5},{5,6},{6,7},{7,8},{8,9},{9,10},{10,1... | collective-permute-start | bytes 196616 | tf_op jit(solution)/shard_map/ppermute | solution.py:77
  38.2 6.7 %collective-permute-start.7 = (bf16[1,2,128,128]{2,3,1,0:T(8,128)(2,1)S(1)}, bf16[1,2,128,128]{2,3,1,0:T(8,128)(2,1)S(1)}, u32[]{:S(2)}, u32[]{:S(2)}) collective-permute-start(bf16[1,2,128,128]{2,3,1,0:T(8,128)(2,1)S(1)} %collective-permute-done.5), channel_id=1, source_target_pairs={{0,15},{1,0},{2,1},{3,2},{4,3},{5,4},{6,5},{7,6},{8,7},{9,8},{10,9... | collective-permute-start | bytes 196616 | tf_op jit(solution)/shard_map/ppermute | solution.py:80
  38.3 6.5 %collective-permute-start.6 = (bf16[1,2,128,128]{2,3,1,0:T(8,128)(2,1)S(1)}, bf16[1,2,128,128]{2,3,1,0:T(8,128)(2,1)S(1)}, u32[]{:S(2)}, u32[]{:S(2)}) collective-permute-start(bf16[1,2,128,128]{2,3,1,0:T(8,128)(2,1)S(1)} %collective-permute-done.4), channel_id=1, source_target_pairs={{0,1},{1,2},{2,3},{3,4},{4,5},{5,6},{6,7},{7,8},{8,9},{9,10},{10,1... | collective-permute-start | bytes 196616 | tf_op jit(solution)/shard_map/ppermute | solution.py:77
  45.0 6.7 %collective-permute-start.9 = (bf16[1,2,128,128]{2,3,1,0:T(8,128)(2,1)S(1)}, bf16[1,2,128,128]{2,3,1,0:T(8,128)(2,1)S(1)}, u32[]{:S(2)}, u32[]{:S(2)}) collective-permute-start(bf16[1,2,128,128]{2,3,1,0:T(8,128)(2,1)S(1)} %collective-permute-done.7), channel_id=1, source_target_pairs={{0,15},{1,0},{2,1},{3,2},{4,3},{5,4},{6,5},{7,6},{8,7},{9,8},{10,9... | collective-permute-start | bytes 196616 | tf_op jit(solution)/shard_map/ppermute | solution.py:80
  45.1 6.5 %collective-permute-start.8 = (bf16[1,2,128,128]{2,3,1,0:T(8,128)(2,1)S(1)}, bf16[1,2,128,128]{2,3,1,0:T(8,128)(2,1)S(1)}, u32[]{:S(2)}, u32[]{:S(2)}) collective-permute-start(bf16[1,2,128,128]{2,3,1,0:T(8,128)(2,1)S(1)} %collective-permute-done.6), channel_id=1, source_target_pairs={{0,1},{1,2},{2,3},{3,4},{4,5},{5,6},{6,7},{7,8},{8,9},{9,10},{10,1... | collective-permute-start | bytes 196616 | tf_op jit(solution)/shard_map/ppermute | solution.py:77
  51.9 6.7 %collective-permute-start.11 = (bf16[1,2,128,128]{2,3,1,0:T(8,128)(2,1)S(1)}, bf16[1,2,128,128]{2,3,1,0:T(8,128)(2,1)S(1)}, u32[]{:S(2)}, u32[]{:S(2)}) collective-permute-start(bf16[1,2,128,128]{2,3,1,0:T(8,128)(2,1)S(1)} %collective-permute-done.9), channel_id=1, source_target_pairs={{0,15},{1,0},{2,1},{3,2},{4,3},{5,4},{6,5},{7,6},{8,7},{9,8},{10,9... | collective-permute-start | bytes 196616 | tf_op jit(solution)/shard_map/ppermute | solution.py:80
  52.0 6.5 %collective-permute-start.10 = (bf16[1,2,128,128]{2,3,1,0:T(8,128)(2,1)S(1)}, bf16[1,2,128,128]{2,3,1,0:T(8,128)(2,1)S(1)}, u32[]{:S(2)}, u32[]{:S(2)}) collective-permute-start(bf16[1,2,128,128]{2,3,1,0:T(8,128)(2,1)S(1)} %collective-permute-done.8), channel_id=1, source_target_pairs={{0,1},{1,2},{2,3},{3,4},{4,5},{5,6},{6,7},{7,8},{8,9},{9,10},{10,1... | collective-permute-start | bytes 196616 | tf_op jit(solution)/shard_map/ppermute | solution.py:77
  58.7 6.7 %collective-permute-start.13 = (bf16[1,2,128,128]{2,3,1,0:T(8,128)(2,1)S(1)}, bf16[1,2,128,128]{2,3,1,0:T(8,128)(2,1)S(1)}, u32[]{:S(2)}, u32[]{:S(2)}) collective-permute-start(bf16[1,2,128,128]{2,3,1,0:T(8,128)(2,1)S(1)} %collective-permute-done.11), channel_id=1, source_target_pairs={{0,15},{1,0},{2,1},{3,2},{4,3},{5,4},{6,5},{7,6},{8,7},{9,8},{10,9... | collective-permute-start | bytes 196616 | tf_op jit(solution)/shard_map/ppermute | solution.py:80
  58.8 6.4 %collective-permute-start.12 = (bf16[1,2,128,128]{2,3,1,0:T(8,128)(2,1)S(1)}, bf16[1,2,128,128]{2,3,1,0:T(8,128)(2,1)S(1)}, u32[]{:S(2)}, u32[]{:S(2)}) collective-permute-start(bf16[1,2,128,128]{2,3,1,0:T(8,128)(2,1)S(1)} %collective-permute-done.10), channel_id=1, source_target_pairs={{0,1},{1,2},{2,3},{3,4},{4,5},{5,6},{6,7},{7,8},{8,9},{9,10},{10,1... | collective-permute-start | bytes 196616 | tf_op jit(solution)/shard_map/ppermute | solution.py:77
  65.4 6.4 %collective-permute-start.14 = (bf16[1,2,128,128]{2,3,1,0:T(8,128)(2,1)S(1)}, bf16[1,2,128,128]{2,3,1,0:T(8,128)(2,1)S(1)}, u32[]{:S(2)}, u32[]{:S(2)}) collective-permute-start(bf16[1,2,128,128]{2,3,1,0:T(8,128)(2,1)S(1)} %collective-permute-done.12), channel_id=1, source_target_pairs={{0,1},{1,2},{2,3},{3,4},{4,5},{5,6},{6,7},{7,8},{8,9},{9,10},{10,1... | collective-permute-start | bytes 196616 | tf_op jit(solution)/shard_map/ppermute | solution.py:77
  73.6 1.7 %copy-start = (bf16[16,2,128,128]{3,2,1,0:T(8,128)(2,1)S(1)}, bf16[16,2,128,128]{3,2,1,0:T(8,128)(2,1)}, u32[]{:S(2)}) copy-start(bf16[16,2,128,128]{3,2,1,0:T(8,128)(2,1)} %param.8) | copy-start | bytes 3145732
  75.3 1.6 %copy-start.1 = (bf16[16,2,128,128]{3,2,1,0:T(8,128)(2,1)S(1)}, bf16[16,2,128,128]{3,2,1,0:T(8,128)(2,1)}, u32[]{:S(2)}) copy-start(bf16[16,2,128,128]{3,2,1,0:T(8,128)(2,1)} %gather_fusion) | copy-start | bytes 3145732
  76.8 1.2 %copy-start.2 = (bf16[16,2,128,128]{3,2,1,0:T(8,128)(2,1)S(1)}, bf16[16,2,128,128]{3,2,1,0:T(8,128)(2,1)}, u32[]{:S(2)}) copy-start(bf16[16,2,128,128]{3,2,1,0:T(8,128)(2,1)} %gather_fusion.1) | copy-start | bytes 3145732
